TPU v7x, 32 devices: a whole 2x2x4 slice. The times are simulated.
32 devices in a mesh: seq: 4 (over y, x), fsdp: 8 (over z, core).
Axes of the slice: x: 2, y: 2, z: 4, core: 2. Of those that a mesh axis runs over, the one named last changes fastest.
Arguments:
- tokens: bfloat16 [8, 1536, 1024], P('fsdp', 'seq'), may hold values from -6 to 6
- segment_ids: int32 [8, 1536], P('fsdp', 'seq'), may hold values from 0 to 5, never falling along the last dimension, each value on 1 to 768 neighbouring positions
- random_blocks: int32 [16, 22, 3], P('seq'), may hold values from 1 to 22, as said below
- ln1_gain: bfloat16 [1024], P('fsdp'), may hold values from 0.099609375 to 1.8984375
- ln1_bias: bfloat16 [1024], P('fsdp'), may hold values from -4 to 4
- w_qkv: bfloat16 [1024, 3072], P('fsdp'), may hold values from -0.25 to 0.25
- w_out: bfloat16 [1024, 1024], P('fsdp'), may hold values from -0.5 to 0.5
- ln2_gain: bfloat16 [1024], P('fsdp'), may hold values from 0.099609375 to 1.8984375
- ln2_bias: bfloat16 [1024], P('fsdp'), may hold values from -4 to 4
- w_in: bfloat16 [1024, 4096], P('fsdp'), may hold values from -0.1875 to 0.1875
- b_in: bfloat16 [4096], P('fsdp'), may hold values from -4 to 4
- w_down: bfloat16 [4096, 1024], P('fsdp'), may hold values from -0.09375 to 0.09375
- b_down: bfloat16 [1024], P('fsdp'), may hold values from -4 to 4
- cotangent: bfloat16 [8, 1536, 1024], P('fsdp', 'seq'), may hold values from -6 to 6
Outputs:
- output: bfloat16 [8, 1536, 1024], P('fsdp', 'seq')
- grad_tokens: bfloat16 [8, 1536, 1024], P('fsdp', 'seq')
- grad_ln1_gain: float32 [1024], P('fsdp')
- grad_ln1_bias: float32 [1024], P('fsdp')
- grad_qkv: float32 [1024, 3072], P('fsdp')
- grad_out_proj: float32 [1024, 1024], P('fsdp')
- grad_ln2_gain: float32 [1024], P('fsdp')
- grad_ln2_bias: float32 [1024], P('fsdp')
- grad_in: float32 [1024, 4096], P('fsdp')
- grad_in_bias: float32 [4096], P('fsdp')
- grad_down: float32 [4096, 1024], P('fsdp')
- grad_down_bias: float32 [1024], P('fsdp')
Inputs may be any that keep to these rules, and one draw needn't show every extreme that they name: For head h and query block b + 1, the 3 entries random_blocks[h, b, :] are different key blocks, none of them 0, 23, b, b + 1 or b + 2. `segment_ids`: in each sequence the segment numbers start at 0, never fall and take every value up to 5; a document has at most 768 tokens, and some document has exactly that many.
All inputs are finite; a program needn't handle non-finite values.
Results may differ from a plain program's by a relative error of at most 0.014.
Values may be sent and summed in bfloat16 or wider, within the bound.
A program may use at most 256 MiB of HBM per device.

v0:
```python
import math
import jax
import jax.numpy as jnp
from jax import lax
from jax.sharding import PartitionSpec as P

DH = 64
BLK = 64


def build_lists(random_blocks, blocks):
    middle_ids = jnp.arange(1, blocks - 1, dtype=jnp.int32)
    head_count = random_blocks.shape[0]
    window_ids = jnp.stack([middle_ids - 1, middle_ids, middle_ids + 1], axis=-1)
    global_ids = jnp.stack(
        [jnp.zeros_like(middle_ids), jnp.full_like(middle_ids, blocks - 1)], axis=-1
    )
    block_list = jnp.concatenate(
        [
            jnp.broadcast_to(window_ids, (head_count, blocks - 2, 3)),
            random_blocks,
            jnp.broadcast_to(global_ids, (head_count, blocks - 2, 2)),
        ],
        axis=-1,
    )
    usable = jnp.concatenate(
        [
            jnp.ones((blocks - 2, 3 + random_blocks.shape[2]), dtype=bool),
            (middle_ids != 1)[:, None],
            (middle_ids != blocks - 2)[:, None],
        ],
        axis=-1,
    )
    return (block_list, usable)


def masked_softmax(scores, allowed):
    shifted = jnp.where(allowed, scores, -1e30)
    top_score = jnp.max(shifted, axis=-1, keepdims=True)
    log_total = top_score + jnp.log(jnp.sum(jnp.exp(shifted - top_score), axis=-1, keepdims=True))
    return (jnp.exp(shifted - log_total), log_total)


def layer_norm(token_rows, gain_vec, bias_vec):
    center = token_rows - jnp.mean(token_rows, axis=-1, keepdims=True)
    variance = jnp.mean(center * center, axis=-1, keepdims=True)
    return center * lax.rsqrt(variance + 1e-05) * gain_vec + bias_vec


def gelu_tanh(pre_act):
    return (
        0.5
        * pre_act
        * (1.0 + jnp.tanh(0.7978845608028654 * (pre_act + 0.044715 * pre_act * pre_act * pre_act)))
    )


def lead_dot(left_arr, right_arr):
    return lax.dot_general(
        left_arr, right_arr, (((0,), (0,)), ((), ())), preferred_element_type=jnp.float32
    )


def last_dot(left_arr, right_arr):
    return lax.dot_general(
        left_arr, right_arr, (((1,), (1,)), ((), ())), preferred_element_type=jnp.float32
    )


def head_setup(queries, keys_all, values_all, block_list, usable, segments):
    length = queries.shape[0]
    blocks = length // BLK
    slot_count = block_list.shape[1]
    blocked_queries = queries.reshape(blocks, BLK, DH)
    neighbour_keys = keys_all.reshape(blocks, BLK, DH)[block_list].reshape(
        blocks - 2, slot_count * BLK, DH
    )
    neighbour_values = values_all.reshape(blocks, BLK, DH)[block_list].reshape(
        blocks - 2, slot_count * BLK, DH
    )
    seg_blocks = segments.reshape(blocks, BLK)
    key_seg = seg_blocks[block_list].reshape(blocks - 2, slot_count * BLK)
    allowed = (seg_blocks[1:-1][:, :, None] == key_seg[:, None, :]) & jnp.repeat(
        usable, BLK, axis=1
    )[:, None, :]
    edge_queries = jnp.concatenate([blocked_queries[0], blocked_queries[-1]], axis=0)
    edge_seg = jnp.concatenate([seg_blocks[0], seg_blocks[-1]], axis=0)
    edge_allowed = edge_seg[:, None] == segments[None, :]
    return (blocked_queries, neighbour_keys, neighbour_values, allowed, edge_queries, edge_allowed)


def head_forward(queries, keys_all, values_all, block_list, usable, segments):
    score_scale = 1.0 / math.sqrt(DH)
    blocked_queries, neighbour_keys, neighbour_values, allowed, edge_queries, edge_allowed = (
        head_setup(queries, keys_all, values_all, block_list, usable, segments)
    )
    unscaled_scores = jnp.einsum(
        "vfn,vmn->vfm", blocked_queries[1:-1], neighbour_keys, preferred_element_type=jnp.float32
    )
    middle_probability, log_mid = masked_softmax(unscaled_scores * score_scale, allowed)
    middle_output = jnp.einsum(
        "icf,ifl->icl",
        middle_probability.astype(jnp.bfloat16),
        neighbour_values,
        preferred_element_type=jnp.float32,
    )
    edge_raw = last_dot(edge_queries, keys_all)
    prob_edge, log_edge = masked_softmax(edge_raw * score_scale, edge_allowed)
    out_edge = jnp.dot(
        prob_edge.astype(jnp.bfloat16), values_all, preferred_element_type=jnp.float32
    )
    merged = jnp.concatenate(
        [out_edge[:BLK], middle_output.reshape(-1, DH), out_edge[BLK:]], axis=0
    )
    return (merged, log_mid, log_edge)


def head_backward(
    queries, keys_all, values_all, block_list, log_mid, log_edge, grad_out, usable, segments
):
    score_scale = 1.0 / math.sqrt(DH)
    length = queries.shape[0]
    blocks = length // BLK
    slot_count = block_list.shape[1]
    blocked_queries, neighbour_keys, neighbour_values, allowed, edge_queries, edge_allowed = (
        head_setup(queries, keys_all, values_all, block_list, usable, segments)
    )
    unscaled_scores = jnp.einsum(
        "vfn,vmn->vfm", blocked_queries[1:-1], neighbour_keys, preferred_element_type=jnp.float32
    )
    middle_probability = jnp.exp(jnp.where(allowed, unscaled_scores * score_scale, -1e30) - log_mid)
    middle_lower_precision = middle_probability.astype(jnp.bfloat16)
    grad_blocks = grad_out.reshape(blocks, BLK, DH)
    middle_block_gradient = grad_blocks[1:-1]
    grad_prob = jnp.einsum(
        "vfn,vmn->vfm", middle_block_gradient, neighbour_values, preferred_element_type=jnp.float32
    )
    delta_mid = jnp.sum(grad_prob * middle_probability, axis=-1, keepdims=True)
    score_gradient = (middle_probability * (grad_prob - delta_mid) * score_scale).astype(
        jnp.bfloat16
    )
    grad_query_mid = jnp.einsum(
        "icf,ifl->icl", score_gradient, neighbour_keys, preferred_element_type=jnp.float32
    )
    near_shape = (blocks - 2, slot_count, BLK, DH)
    grad_near_keys = jnp.einsum(
        "onm,ons->oms", score_gradient, blocked_queries[1:-1], preferred_element_type=jnp.float32
    ).reshape(near_shape)
    grad_near_values = jnp.einsum(
        "onm,ons->oms",
        middle_lower_precision,
        middle_block_gradient,
        preferred_element_type=jnp.float32,
    ).reshape(near_shape)
    edge_raw = last_dot(edge_queries, keys_all)
    prob_edge = jnp.exp(jnp.where(edge_allowed, edge_raw * score_scale, -1e30) - log_edge)
    edge_low = prob_edge.astype(jnp.bfloat16)
    grad_edge = jnp.concatenate([grad_blocks[0], grad_blocks[-1]], axis=0)
    grad_edge_prob = last_dot(grad_edge, values_all)
    delta_edge = jnp.sum(grad_edge_prob * prob_edge, axis=-1, keepdims=True)
    grad_edge_scores = (prob_edge * (grad_edge_prob - delta_edge) * score_scale).astype(
        jnp.bfloat16
    )
    grad_query_edge = jnp.dot(grad_edge_scores, keys_all, preferred_element_type=jnp.float32)
    grad_keys = (
        lead_dot(grad_edge_scores, edge_queries)
        .reshape(blocks, BLK, DH)
        .at[block_list]
        .add(grad_near_keys)
    )
    grad_values = (
        lead_dot(edge_low, grad_edge).reshape(blocks, BLK, DH).at[block_list].add(grad_near_values)
    )
    grad_queries = jnp.concatenate(
        [grad_query_edge[:BLK], grad_query_mid.reshape(-1, DH), grad_query_edge[BLK:]], axis=0
    )
    return jnp.stack(
        [grad_queries, grad_keys.reshape(-1, DH), grad_values.reshape(-1, DH)], axis=0
    ).astype(jnp.bfloat16)


def per_device(
    tokens,
    segment_ids,
    random_blocks,
    ln1_gain,
    ln1_bias,
    w_qkv,
    w_out,
    ln2_gain,
    ln2_bias,
    w_in,
    b_in,
    w_down,
    b_down,
    cotangent,
):
    gain_one, bias_one, qkv_weight, out_weight = (
        lax.all_gather(ln1_gain, "fsdp", axis=0, tiled=True),
        lax.all_gather(ln1_bias, "fsdp", axis=0, tiled=True),
        lax.all_gather(w_qkv, "fsdp", axis=0, tiled=True),
        lax.all_gather(w_out, "fsdp", axis=0, tiled=True),
    )
    gain_two, bias_two, in_weight, in_bias, down_weight, down_bias = (
        lax.all_gather(ln2_gain, "fsdp", axis=0, tiled=True),
        lax.all_gather(ln2_bias, "fsdp", axis=0, tiled=True),
        lax.all_gather(w_in, "fsdp", axis=0, tiled=True),
        lax.all_gather(b_in, "fsdp", axis=0, tiled=True),
        lax.all_gather(w_down, "fsdp", axis=0, tiled=True),
        lax.all_gather(b_down, "fsdp", axis=0, tiled=True),
    )
    token_rows = tokens[0].astype(jnp.float32)
    tok_count, width = token_rows.shape
    norm_one, pull_one = jax.vjp(
        layer_norm, token_rows, gain_one.astype(jnp.float32), bias_one.astype(jnp.float32)
    )
    normed_one = norm_one.astype(jnp.bfloat16)
    qkv_rows = (
        jnp.dot(normed_one, qkv_weight, preferred_element_type=jnp.float32)
        .astype(jnp.bfloat16)
        .reshape(tok_count, 3, width)
    )
    by_heads = lax.all_to_all(qkv_rows, "seq", split_axis=2, concat_axis=0, tiled=True)
    seq_ids = lax.all_gather(segment_ids[0], "seq", axis=0, tiled=True)
    length = by_heads.shape[0]
    head_count = random_blocks.shape[0]
    head_split = by_heads.reshape(length, 3, head_count, DH).transpose(1, 2, 0, 3)
    block_list, usable = build_lists(random_blocks, length // BLK)

    def forward_head(operands):
        return head_forward(operands[0], operands[1], operands[2], operands[3], usable, seq_ids)

    head_out, log_mid, log_edge = lax.map(
        forward_head, (head_split[0], head_split[1], head_split[2], block_list)
    )
    att_heads = head_out.transpose(1, 0, 2).reshape(length, head_count * DH).astype(jnp.bfloat16)
    att_rows = lax.all_to_all(att_heads, "seq", split_axis=0, concat_axis=1, tiled=True)
    branch = jnp.dot(att_rows, out_weight, preferred_element_type=jnp.float32)
    hidden = token_rows + branch
    norm_two, pull_two = jax.vjp(
        layer_norm, hidden, gain_two.astype(jnp.float32), bias_two.astype(jnp.float32)
    )
    normed_two = norm_two.astype(jnp.bfloat16)
    pre_act = jnp.dot(normed_two, in_weight, preferred_element_type=jnp.float32) + in_bias.astype(
        jnp.float32
    )
    act_value, pull_gelu = jax.vjp(gelu_tanh, pre_act)
    act_low = act_value.astype(jnp.bfloat16)
    result = (
        hidden
        + jnp.dot(act_low, down_weight, preferred_element_type=jnp.float32)
        + down_bias.astype(jnp.float32)
    )
    cot_low = cotangent[0]
    cot_rows = cot_low.astype(jnp.float32)
    in_back, down_back = (
        lax.all_gather(w_in, "fsdp", axis=0, tiled=True),
        lax.all_gather(w_down, "fsdp", axis=0, tiled=True),
    )
    grad_down = lead_dot(act_low, cot_low)
    grad_down_bias = jnp.sum(cot_rows, axis=0)
    grad_act = last_dot(cot_low, down_back)
    grad_pre = pull_gelu(grad_act)[0].astype(jnp.bfloat16)
    grad_in = lead_dot(normed_two, grad_pre)
    grad_in_bias = jnp.sum(grad_pre.astype(jnp.float32), axis=0)
    grad_norm_two = last_dot(grad_pre, in_back)
    grad_hidden_norm, grad_gain_two, grad_bias_two = pull_two(grad_norm_two)
    grad_hidden = cot_rows + grad_hidden_norm
    ffn_shares = (
        lax.psum_scatter(grad_gain_two, "fsdp", scatter_dimension=0, tiled=True),
        lax.psum_scatter(grad_bias_two, "fsdp", scatter_dimension=0, tiled=True),
        lax.psum_scatter(grad_in, "fsdp", scatter_dimension=0, tiled=True),
        lax.psum_scatter(grad_in_bias, "fsdp", scatter_dimension=0, tiled=True),
        lax.psum_scatter(grad_down, "fsdp", scatter_dimension=0, tiled=True),
        lax.psum_scatter(grad_down_bias, "fsdp", scatter_dimension=0, tiled=True),
    )
    qkv_back, out_back = (
        lax.all_gather(w_qkv, "fsdp", axis=0, tiled=True),
        lax.all_gather(w_out, "fsdp", axis=0, tiled=True),
    )
    hidden_low = grad_hidden.astype(jnp.bfloat16)
    grad_out_proj = lead_dot(att_rows, hidden_low)
    grad_att = last_dot(hidden_low, out_back).astype(jnp.bfloat16)
    grad_att_heads = lax.all_to_all(grad_att, "seq", split_axis=1, concat_axis=0, tiled=True)
    grad_split = grad_att_heads.reshape(length, head_count, DH).transpose(1, 0, 2)

    def backward_head(operands):
        return head_backward(
            operands[0],
            operands[1],
            operands[2],
            operands[3],
            operands[4],
            operands[5],
            operands[6],
            usable,
            seq_ids,
        )

    head_grads = lax.map(
        backward_head,
        (head_split[0], head_split[1], head_split[2], block_list, log_mid, log_edge, grad_split),
    )
    grad_heads = head_grads.transpose(2, 1, 0, 3).reshape(length, 3, head_count * DH)
    grad_qkv_rows = lax.all_to_all(
        grad_heads, "seq", split_axis=0, concat_axis=2, tiled=True
    ).reshape(tok_count, 3 * width)
    grad_qkv = lead_dot(normed_one, grad_qkv_rows)
    grad_norm_one = last_dot(grad_qkv_rows, qkv_back)
    grad_rows_norm, grad_gain_one, grad_bias_one = pull_one(grad_norm_one)
    grad_tokens = (grad_hidden + grad_rows_norm).astype(jnp.bfloat16)[None]
    attn_shares = (
        lax.psum_scatter(grad_gain_one, "fsdp", scatter_dimension=0, tiled=True),
        lax.psum_scatter(grad_bias_one, "fsdp", scatter_dimension=0, tiled=True),
        lax.psum_scatter(grad_qkv, "fsdp", scatter_dimension=0, tiled=True),
        lax.psum_scatter(grad_out_proj, "fsdp", scatter_dimension=0, tiled=True),
    )
    shares = attn_shares + ffn_shares
    totals = lax.psum(
        (
            shares[0],
            shares[1],
            shares[2],
            shares[3],
            shares[4],
            shares[5],
            shares[6],
            shares[7],
            shares[8],
            shares[9],
        ),
        "seq",
    )
    return (
        result.astype(jnp.bfloat16)[None],
        grad_tokens,
        totals[0],
        totals[1],
        totals[2],
        totals[3],
        totals[4],
        totals[5],
        totals[6],
        totals[7],
        totals[8],
        totals[9],
    )


def solution(mesh):
    return jax.shard_map(
        per_device,
        mesh=mesh,
        in_specs=(
            P("fsdp", "seq", None),
            P("fsdp", "seq"),
            P("seq", None, None),
            P("fsdp"),
            P("fsdp"),
            P("fsdp", None),
            P("fsdp", None),
            P("fsdp"),
            P("fsdp"),
            P("fsdp", None),
            P("fsdp"),
            P("fsdp", None),
            P("fsdp"),
            P("fsdp", "seq", None),
        ),
        out_specs=(
            P("fsdp", "seq", None),
            P("fsdp", "seq", None),
            P("fsdp"),
            P("fsdp"),
            P("fsdp", None),
            P("fsdp", None),
            P("fsdp"),
            P("fsdp"),
            P("fsdp", None),
            P("fsdp"),
            P("fsdp", None),
            P("fsdp"),
        ),
        check_vma=False,
    )
```

profile of v0, /device:TPU:0, one launch (start us, length us, event | category | flops | bytes accessed | tf_op | source)
XLA Modules:
  0.0 1317.8 jit_solution(9193868924157783332)
XLA Ops:
  9.4 13.5 %all-gather.1 = bf16[8,1,128]{2,1,0:T(2,128)(2,1)S(1)} all-gather(bf16[1,1,128]{2,1,0:T(2,128)(2,1)} %bitcast.348), channel_id=1, replica_groups=mesh['seq'=4,'fsdp'=8] {'fsdp'}, dimensions={0}, use_global_device_ids=true | all-gather | bytes 2304 | tf_op jit(solution)/shard_map/all_gather | solution.py:199
  23.0 8.8 all-gather.2
  34.1 43.1 %all-gather.12.cloned.1.call-done = bf16[1024,3072]{1,0:T(8,128)(2,1)} async-done(((bf16[128,3072]{1,0:T(8,128)(2,1)}), bf16[1024,3072]{1,0:T(8,128)(2,1)}) %all-gather.12.cloned.1.call-update) | async-done | bytes 6291472 | tf_op jit(solution)/shard_map/all_gather | solution.py:201
  95.5 39.0 %all-gather = s32[1,1536]{1,0:T(1,128)S(1)} all-gather(s32[1,384]{1,0:T(1,128)S(1)} %copy-done.53), channel_id=2, replica_groups=mesh['seq'=4,'fsdp'=8] {'seq'}, dimensions={1}, use_global_device_ids=true | all-gather | bytes 7680 | tf_op jit(solution)/shard_map/all_gather | solution.py:224
  149.5 64.8 %while.26 = (s32[]{:T(128)}, bf16[4,1536,64]{2,1,0:T(8,128)(2,1)}, f32[4,22,64,1]{2,1,3,0:T(8,128)}, f32[4,128,1]{1,2,0:T(1,128)}, s32[128]{0:T(128)S(1)}, /*ind...) while((s32[]{:T(128)}, bf16[4,1536,64]{2,1,0:T(8,128)(2,1)}, ...), condition=%wide.region_7.8_spmd, body=%wide.region_2.7_spmd.sunk | while | flops 243564560 | bytes 28432796 | solution.py:233
  220.7 9.3 all-gather.3
  230.1 10.3 all-gather.4
  240.4 12.9 all-gather.5
  256.4 9.3 convolution_add_fusion
  271.9 11.9 convert_reduce_fusion
  309.3 333.9 %while.27 = (s32[]{:T(128)}, bf16[4,3,1536,64]{2,3,0,1:T(8,128)(2,1)}, s32[128]{0:T(128)S(1)}, s32[1536]{0:T(1024)S(1)}, bf16[4,1536,64]{2,1,0:T(8,128)(2,1)}, /...) while((s32[]{:T(128)}, ...), condition=%wide.region_17.18_spmd, body=%wide.region_12.17_spmd.sunk | while | flops 603952256 | bytes 75161568 | solution.py:300
  340.6 8.3 fusion.198
  348.9 18.4 %scatter_fusion.1 = f32[24,64,64]{2,1,0:T(8,128)S(1)} fusion(f32[24,64,64]{2,1,0:T(8,128)S(1)} %bitcast.297, s32[176]{0:T(256)S(1)} %reshape.627, f32[176,64,64]{2,1,0:T(8,128)} %bitcast.303), kind=kCustom, calls=%fused_computation.6.clone.1 | custom fusion | flops 720896 | bytes 8651456 | tf_op jit(solution)/shard_map/while/body/eval_jaxpr/scatter-add | solution.py:169
  372.6 18.4 %scatter_fusion = f32[24,64,64]{2,1,0:T(8,128)S(1)} fusion(f32[24,64,64]{2,1,0:T(8,128)S(1)} %bitcast.296, s32[176]{0:T(256)S(1)} %reshape.627, f32[176,64,64]{2,1,0:T(8,128)} %bitcast.302), kind=kCustom, calls=%fused_computation.7.clone.1 | custom fusion | flops 720896 | bytes 8651456 | tf_op jit(solution)/shard_map/while/body/eval_jaxpr/scatter-add | solution.py:172
  424.1 8.3 fusion.198
  432.3 18.4 %scatter_fusion.1 = f32[24,64,64]{2,1,0:T(8,128)S(1)} fusion(f32[24,64,64]{2,1,0:T(8,128)S(1)} %bitcast.297, s32[176]{0:T(256)S(1)} %reshape.627, f32[176,64,64]{2,1,0:T(8,128)} %bitcast.303), kind=kCustom, calls=%fused_computation.6.clone.1 | custom fusion | flops 720896 | bytes 8651456 | tf_op jit(solution)/shard_map/while/body/eval_jaxpr/scatter-add | solution.py:169
  456.1 18.4 %scatter_fusion = f32[24,64,64]{2,1,0:T(8,128)S(1)} fusion(f32[24,64,64]{2,1,0:T(8,128)S(1)} %bitcast.296, s32[176]{0:T(256)S(1)} %reshape.627, f32[176,64,64]{2,1,0:T(8,128)} %bitcast.302), kind=kCustom, calls=%fused_computation.7.clone.1 | custom fusion | flops 720896 | bytes 8651456 | tf_op jit(solution)/shard_map/while/body/eval_jaxpr/scatter-add | solution.py:172
  515.8 18.4 %scatter_fusion.1 = f32[24,64,64]{2,1,0:T(8,128)S(1)} fusion(f32[24,64,64]{2,1,0:T(8,128)S(1)} %bitcast.297, s32[176]{0:T(256)S(1)} %reshape.627, f32[176,64,64]{2,1,0:T(8,128)} %bitcast.303), kind=kCustom, calls=%fused_computation.6.clone.1 | custom fusion | flops 720896 | bytes 8651456 | tf_op jit(solution)/shard_map/while/body/eval_jaxpr/scatter-add | solution.py:169
  539.6 18.4 %scatter_fusion = f32[24,64,64]{2,1,0:T(8,128)S(1)} fusion(f32[24,64,64]{2,1,0:T(8,128)S(1)} %bitcast.296, s32[176]{0:T(256)S(1)} %reshape.627, f32[176,64,64]{2,1,0:T(8,128)} %bitcast.302), kind=kCustom, calls=%fused_computation.7.clone.1 | custom fusion | flops 720896 | bytes 8651456 | tf_op jit(solution)/shard_map/while/body/eval_jaxpr/scatter-add | solution.py:172
  599.3 18.4 %scatter_fusion.1 = f32[24,64,64]{2,1,0:T(8,128)S(1)} fusion(f32[24,64,64]{2,1,0:T(8,128)S(1)} %bitcast.297, s32[176]{0:T(256)S(1)} %reshape.627, f32[176,64,64]{2,1,0:T(8,128)} %bitcast.303), kind=kCustom, calls=%fused_computation.6.clone.1 | custom fusion | flops 720896 | bytes 8651456 | tf_op jit(solution)/shard_map/while/body/eval_jaxpr/scatter-add | solution.py:169
  623.0 18.4 %scatter_fusion = f32[24,64,64]{2,1,0:T(8,128)S(1)} fusion(f32[24,64,64]{2,1,0:T(8,128)S(1)} %bitcast.296, s32[176]{0:T(256)S(1)} %reshape.627, f32[176,64,64]{2,1,0:T(8,128)} %bitcast.302), kind=kCustom, calls=%fused_computation.7.clone.1 | custom fusion | flops 720896 | bytes 8651456 | tf_op jit(solution)/shard_map/while/body/eval_jaxpr/scatter-add | solution.py:172
  647.5 38.9 %all_to_all.62 = bf16[1536,3,256]{2,1,0:T(4,128)(2,1)S(1)} all-to-all(bf16[1536,3,256]{2,1,0:T(4,128)(2,1)S(1)} %copy.189), channel_id=1, replica_groups=mesh['seq'=4,'fsdp'=8] {'seq'}, dimensions={0} | all-to-all | bytes 4718592 | tf_op jit(solution)/shard_map/all_to_all | solution.py:305
  699.3 12.3 fusion.78
  713.0 10.2 fusion.95
  723.3 101.4 %reduce-scatter.5.cloned.1.call-done = f32[128,3072]{1,0:T(8,128)} async-done(((f32[1024,3072]{1,0:T(8,128)}), f32[128,3072]{1,0:T(8,128)}) %reduce-scatter.5.cloned.1.call-update) | async-done | bytes 1572880 | tf_op jit(solution)/shard_map/reduce_scatter | solution.py:315
  824.7 169.0 %reduce-scatter.11.cloned.1.call-done = f32[512,1024]{1,0:T(8,128)} async-done(((f32[4096,1024]{1,0:T(8,128)}), f32[512,1024]{1,0:T(8,128)}) %reduce-scatter.11.cloned.1.call-update) | async-done | bytes 2097168 | tf_op jit(solution)/shard_map/reduce_scatter | solution.py:274
  993.7 169.0 %reduce-scatter.9.cloned.1.call-done = f32[128,4096]{1,0:T(8,128)} async-done(((f32[1024,4096]{1,0:T(8,128)}), f32[128,4096]{1,0:T(8,128)}) %reduce-scatter.9.cloned.1.call-update) | async-done | bytes 2097168 | tf_op jit(solution)/shard_map/reduce_scatter | solution.py:272
  1165.2 9.3 all-gather.6
  1174.6 10.5 fusion.71
  1193.6 26.7 %all-reduce.6 = (f32[1024]{0:T(1024)S(1)}, f32[1024]{0:T(1024)S(1)}, f32[1024]{0:T(1024)S(1)}, f32[1024]{0:T(1024)S(1)}, f32[4096]{0:T(1024)S(1)}, /*index=5*/f32[1024]{0:T(1024)S(1)}) all-reduce(f32[1024]{0:T(1024)S(1)} %get-tuple-element.315, f32[1024]{0:T(1024)S(1)} %get-tuple-element.318, ...), channel_id=3, replica_groups=mesh['seq'=4,'fsdp'=8] {'fsdp'}, use_global_device_ids=true, to_apply=%region_21.22.clone | all-reduce | flops 9216 | bytes 73728
  1220.7 11.4 all-reduce.7
  1232.1 72.6 %all-reduce.11.cloned.1.call-done = (f32[128,3072]{1,0:T(8,128)}, f32[128,1024]{1,0:T(8,128)}, f32[128,4096]{1,0:T(8,128)}, f32[512,1024]{1,0:T(8,128)}) async-done(((f32[128,3072]{1,0:T(8,128)}, f32[128,1024]{1,0:T(8,128)}, f32[128,4096]{1,0:T(8,128)}, f32[512,1024]{1,0:T(8,128)}), (f32[128,3072]{1,0:T(8,128)}, f32[128,1024]{1,0:T(8,128)}, f32[128,4096]{1,0:T(8,128)}, ...) | async-done | bytes 6291472 | tf_op jit(solution)/shard_map/psum | solution.py:319
  (574 shorter events, 347.3 us)
Async XLA Ops:
  7.2 26.0 %copy-start.2 = (bf16[1,384,1024]{2,1,0:T(8,128)(2,1)S(1)}, bf16[1,384,1024]{2,1,0:T(8,128)(2,1)}, u32[]{:S(2)}) copy-start(bf16[1,384,1024]{2,1,0:T(8,128)(2,1)} %param.18) | copy-start | bytes 2359300
  7.2 70.0 %all-gather.12.cloned.1.call-start = ((), (), s32[]{:S(2)}) async-start(), calls=%async_computation.8 | async-start | bytes 7077888 | tf_op jit(solution)/shard_map/all_gather | solution.py:201
  7.9 245.4 %all-gather.14.cloned.1.call-start = ((), (), s32[]{:S(2)}) async-start(), calls=%async_computation.9 | async-start | bytes 2359296 | tf_op jit(solution)/shard_map/all_gather | solution.py:202
  8.7 247.7 %all-gather.16.cloned.1.call-start = ((), (), s32[]{:S(2)}) async-start(), calls=%async_computation.10 | async-start | bytes 9437184 | tf_op jit(solution)/shard_map/all_gather | solution.py:207
  23.0 54.2 %copy-start.31 = (f32[8,1,128]{2,1,0:T(1,128)}, f32[8,1,128]{2,1,0:T(1,128)S(1)}, u32[]{:S(2)}) copy-start(f32[8,1,128]{2,1,0:T(1,128)S(1)} %convert_element_type.130) | copy-start | bytes 12292
  31.8 45.4 %copy-start.33 = (f32[8,1,128]{2,1,0:T(1,128)}, f32[8,1,128]{2,1,0:T(1,128)S(1)}, u32[]{:S(2)}) copy-start(f32[8,1,128]{2,1,0:T(1,128)S(1)} %convert_element_type.131) | copy-start | bytes 12292
  33.1 44.1 %copy-start.37 = (f32[384]{0:T(512)}, f32[384]{0:T(512)S(1)}, u32[]{:S(2)}) copy-start(f32[384]{0:T(512)S(1)} %broadcast_multiply_fusion.1) | copy-start | bytes 4612
  34.1 43.1 %copy-start.41 = (f32[384]{0:T(512)}, f32[384]{0:T(512)S(1)}, u32[]{:S(2)}) copy-start(f32[384]{0:T(512)S(1)} %fusion.92) | copy-start | bytes 4612
  90.8 43.7 %copy-start.50 = (s32[4,22,3]{1,0,2:T(4,128)S(1)}, s32[4,22,3]{1,0,2:T(4,128)}, u32[]{:S(2)}) copy-start(s32[4,22,3]{1,0,2:T(4,128)} %param.20) | copy-start | bytes 3172
  90.8 43.8 %copy-start.55 = (s32[22,2]{0,1:T(2,128)S(1)}, s32[22,2]{0,1:T(2,128)}, u32[]{:S(2)}) copy-start(s32[22,2]{0,1:T(2,128)} %constant.106.clone.1) | copy-start | bytes 532
  90.8 44.1 %all-to-all-start = ((bf16[384,3,1024]{0,1,2:T(4,128)(2,1)}), bf16[384,3,1024]{0,1,2:T(4,128)(2,1)S(1)}, u32[]{:S(2)}, u32[]{:S(2)}) async-start(bf16[384,3,1024]{0,1,2:T(4,128)(2,1)} %copy.169), calls=%async_computation | async-start | bytes 6291456 | tf_op jit(solution)/shard_map/all_to_all | solution.py:223
  94.6 177.3 %all-gather.18.cloned.1.call-start = ((), (), s32[]{:S(2)}) async-start(), calls=%async_computation.11 | async-start | bytes 9437184 | tf_op jit(solution)/shard_map/all_gather | solution.py:209
  216.0 14.0 %copy-start.57 = (bf16[128]{0:T(256)(128)(2,1)S(1)}, bf16[128]{0:T(256)(128)(2,1)}, u32[]{:S(2)}) copy-start(bf16[128]{0:T(256)(128)(2,1)} %param.26) | copy-start | bytes 772
  216.0 37.3 %copy-start.3 = (bf16[1,384,1024]{2,1,0:T(8,128)(2,1)S(1)}, bf16[1,384,1024]{2,1,0:T(8,128)(2,1)}, u32[]{:S(2)}) copy-start(bf16[1,384,1024]{2,1,0:T(8,128)(2,1)} %param.18) | copy-start | bytes 2359300
  217.2 36.1 %all-to-all-start.1 = ((bf16[4,384,256]{1,2,0:T(8,128)(2,1)}), bf16[4,384,256]{1,2,0:T(8,128)(2,1)S(1)}, u32[]{:S(2)}, u32[]{:S(2)}) async-start(bf16[4,384,256]{1,2,0:T(8,128)(2,1)} %copy.179), calls=%async_computation.1 | async-start | bytes 1572864 | tf_op jit(solution)/shard_map/all_to_all | solution.py:237
  230.1 58.1 %copy-start.22 = (f32[8,1,128]{2,1,0:T(1,128)}, f32[8,1,128]{2,1,0:T(1,128)S(1)}, u32[]{:S(2)}) copy-start(f32[8,1,128]{2,1,0:T(1,128)S(1)} %convert_element_type.132) | copy-start | bytes 12292
  240.3 16.0 %copy-start.26 = (f32[8,1,128]{2,1,0:T(1,128)}, f32[8,1,128]{2,1,0:T(1,128)S(1)}, u32[]{:S(2)}) copy-start(f32[8,1,128]{2,1,0:T(1,128)S(1)} %convert_element_type.133) | copy-start | bytes 12292
  256.0 32.2 %copy-start.5 = (f32[384,1024]{1,0:T(8,128)}, f32[384,1024]{1,0:T(8,128)S(1)}, u32[]{:S(2)}) copy-start(f32[384,1024]{1,0:T(8,128)S(1)} %get-tuple-element.416) | copy-start | bytes 4718596
  256.0 32.2 %copy-start.35 = (f32[384]{0:T(512)}, f32[384]{0:T(512)S(1)}, u32[]{:S(2)}) copy-start(f32[384]{0:T(512)S(1)} %broadcast_multiply_fusion) | copy-start | bytes 4612
  256.3 31.9 %copy-start.39 = (f32[384]{0:T(512)}, f32[384]{0:T(512)S(1)}, u32[]{:S(2)}) copy-start(f32[384]{0:T(512)S(1)} %fusion.93) | copy-start | bytes 4612
  256.4 15.6 %copy-start.12 = (bf16[1,384,1024]{2,1,0:T(8,128)(2,1)S(1)}, bf16[1,384,1024]{2,1,0:T(8,128)(2,1)}, u32[]{:S(2)}) copy-start(bf16[1,384,1024]{2,1,0:T(8,128)(2,1)} %param.31) | copy-start | bytes 2359300
  271.9 11.9 copy-start.59
  292.6 15.0 %all-to-all-start.2 = ((bf16[384,4,256]{0,2,1:T(8,128)(2,1)}), bf16[384,4,256]{0,2,1:T(8,128)(2,1)S(1)}, u32[]{:S(2)}, u32[]{:S(2)}) async-start(bf16[384,4,256]{0,2,1:T(8,128)(2,1)} %bitcast.63), calls=%async_computation.2 | async-start | bytes 1572864 | tf_op jit(solution)/shard_map/all_to_all | solution.py:284
  296.3 427.0 %reduce-scatter.7.cloned.1.call-start = ((), (), s32[]{:S(2)}) async-start(), calls=%async_computation.13 | async-start | bytes 4718592 | tf_op jit(solution)/shard_map/reduce_scatter | solution.py:316
  299.5 525.2 %reduce-scatter.5.cloned.1.call-start = ((), (), s32[]{:S(2)}) async-start(), calls=%async_computation.12 | async-start | bytes 14155776 | tf_op jit(solution)/shard_map/reduce_scatter | solution.py:315
  309.4 10.7 copy-start.48
  392.9 10.7 copy-start.48
  476.4 10.7 copy-start.48
  559.8 10.7 copy-start.48
  698.2 295.6 %reduce-scatter.11.cloned.1.call-start = ((), (), s32[]{:S(2)}) async-start(), calls=%async_computation.15 | async-start | bytes 18874368 | tf_op jit(solution)/shard_map/reduce_scatter | solution.py:274
  711.6 451.1 %reduce-scatter.9.cloned.1.call-start = ((), (), s32[]{:S(2)}) async-start(), calls=%async_computation.14 | async-start | bytes 18874368 | tf_op jit(solution)/shard_map/reduce_scatter | solution.py:272
  723.2 581.5 %all-reduce.11.cloned.1.call-start = ((), (), s32[]{:S(2)}) async-start(), calls=%async_computation.16 | async-start | bytes 12582912 | tf_op jit(solution)/shard_map/psum | solution.py:319
  (77 other events, 289.4 us)
Sparse Core Ops, SparseCore 0:
  9.7 67.4 all-gather.11
  78.8 27.6 all-gather.13
  108.1 81.6 all-gather.15
  191.2 80.6 all-gather.17
  299.6 48.9 reduce-scatter.6
  698.3 126.3 reduce-scatter.4
  827.1 166.6 reduce-scatter.10
  996.1 166.5 reduce-scatter.8
  1166.5 138.2 all-reduce.10
where the time goes:
time: 1330 us; the launch traced here: 1320 us
  waiting for transfers between devices  572 us (43%)
  matrix products  213 us (16%)
  blocking collectives  180 us (14%)
  other arithmetic  168 us (13%)
  local copies, waits for them, and re-layouts  156 us (12%)
  between operations  16 us (1%)
    reduce_scatter x1, waiting for transfers between devices, per_device(): lax.psum_scatter(grad_down, 'fsdp', scatter_dimension=0, tiled=True)  169 us
    reduce_scatter x1, waiting for transfers between devices, per_device(): lax.psum_scatter(grad_in, 'fsdp', scatter_dimension=0, tiled=True)  169 us
    reduce_scatter x1, waiting for transfers between devices, per_device(): lax.psum_scatter(grad_qkv, 'fsdp', scatter_dimension=0, tiled=True)  101 us
    scatter-add x4, other arithmetic, head_backward(): grad_keys = lead_dot(grad_edge_scores, edge_queries).reshape(blocks, BLK,...  73.5 us
    scatter-add x4, other arithmetic, head_backward(): lead_dot(edge_low, grad_edge).reshape(blocks, BLK, DH).at[block_list]  73.5 us
    psum x1, waiting for transfers between devices, per_device(): lax.psum((shares[0], shares[1], shares[2], shares[3], shares[4], shares[5...  72.6 us
    all_gather x1, waiting for transfers between devices, per_device(): lax.all_gather(w_qkv, 'fsdp', axis=0, tiled=True)  43.1 us
    all_gather x1, blocking collectives, per_device(): seq_ids = lax.all_gather(segment_ids[0], 'seq', axis=0, tiled=True)  39 us
  transfers between devices with their start and end apart: 12, of which 7 were waited for; matrix products, arithmetic and copies ran while one was open for 38% of the time, Pallas kernels for 0%

commit v1 on v0

--- a/solution.py
+++ b/solution.py
@@ -221,7 +221,12 @@
         .reshape(tok_count, 3, width)
     )
     by_heads = lax.all_to_all(qkv_rows, "seq", split_axis=2, concat_axis=0, tiled=True)
-    seq_ids = lax.all_gather(segment_ids[0], "seq", axis=0, tiled=True)
+    ring = [segment_ids[0]]
+    for hop in range(3):
+        ring.append(lax.ppermute(ring[-1], "seq", [(dev, (dev + 1) % 4) for dev in range(4)]))
+    seq_ids = jnp.roll(
+        jnp.concatenate(ring[::-1], axis=0), (lax.axis_index("seq") + 1) * ring[0].shape[0], axis=0
+    )
     length = by_heads.shape[0]
     head_count = random_blocks.shape[0]
     head_split = by_heads.reshape(length, 3, head_count, DH).transpose(1, 2, 0, 3)

time: 1330 us -> 1330 us (level)
  blocking collectives: 180 us -> 141 us
  waiting for transfers between devices: 572 us -> 606 us
    ppermute x0 -> x3, waiting for transfers between devices: none -> 39.7 us  [per_device(): lax.ppermute(ring[-1], 'seq', [(dev, (dev + 1) % 4) for dev in range(4)])]
    all_gather x1 -> x0, blocking collectives: 39 us -> none  [per_device(): seq_ids = lax.all_gather(segment_ids[0], 'seq', axis=0, tiled=True)]
  transfers between devices with their start and end apart: 12 -> 15, of which waited for: 7 -> 9; matrix products, arithmetic and copies ran while one was open for 38% -> 38% of each run, Pallas kernels for 0% -> 0%
where the time goes in v1:
time: 1330 us; the launch traced here: 1320 us
  waiting for transfers between devices  606 us (46%)
  matrix products  213 us (16%)
  other arithmetic  167 us (13%)
  local copies, waits for them, and re-layouts  156 us (12%)
  blocking collectives  141 us (11%)
  starting transfers between devices  16.9 us (1%)
  between operations  16.1 us (1%)
    reduce_scatter x1, waiting for transfers between devices, per_device(): lax.psum_scatter(grad_down, 'fsdp', scatter_dimension=0, tiled=True)  169 us
    reduce_scatter x1, waiting for transfers between devices, per_device(): lax.psum_scatter(grad_in, 'fsdp', scatter_dimension=0, tiled=True)  169 us
    reduce_scatter x1, waiting for transfers between devices, per_device(): lax.psum_scatter(grad_qkv, 'fsdp', scatter_dimension=0, tiled=True)  101 us
    scatter-add x4, other arithmetic, head_backward(): grad_keys = lead_dot(grad_edge_scores, edge_queries).reshape(blocks, BLK,...  73.5 us
    scatter-add x4, other arithmetic, head_backward(): lead_dot(edge_low, grad_edge).reshape(blocks, BLK, DH).at[block_list]  73.5 us
    psum x1, waiting for transfers between devices, per_device(): lax.psum((shares[0], shares[1], shares[2], shares[3], shares[4], shares[5...  72.6 us
    all_gather x1, waiting for transfers between devices, per_device(): lax.all_gather(w_qkv, 'fsdp', axis=0, tiled=True)  42 us
    ppermute x3, waiting for transfers between devices, per_device(): lax.ppermute(ring[-1], 'seq', [(dev, (dev + 1) % 4) for dev in range(4)])  39.7 us
  transfers between devices with their start and end apart: 15, of which 9 were waited for; matrix products, arithmetic and copies ran while one was open for 38% of the time, Pallas kernels for 0%

profile of v1, /device:TPU:0, one launch (start us, length us, event | category | flops | bytes accessed | tf_op | source)
XLA Modules:
  0.0 1317.7 jit_solution(15591807896573445334)
XLA Ops:
  14.3 12.0 all-gather
  26.4 8.8 all-gather.1
  35.2 42.0 %all-gather.11.cloned.1.call-done = bf16[1024,3072]{1,0:T(8,128)(2,1)} async-done(((bf16[128,3072]{1,0:T(8,128)(2,1)}), bf16[1024,3072]{1,0:T(8,128)(2,1)}) %all-gather.11.cloned.1.call-update) | async-done | bytes 6291472 | tf_op jit(solution)/shard_map/all_gather | solution.py:201
  96.8 35.6 %collective-permute-done.1 = s32[384]{0:T(512)S(1)} collective-permute-done((s32[384]{0:T(512)S(1)}, s32[384]{0:T(512)S(1)}, u32[]{:S(2)}, u32[]{:S(2)}) %collective-permute-start.1) | collective-permute-done | bytes 1568 | tf_op jit(solution)/shard_map/ppermute | solution.py:226
  152.0 64.9 %while.26 = (s32[]{:T(128)}, bf16[4,1536,64]{2,1,0:T(8,128)(2,1)}, f32[4,22,64,1]{2,1,3,0:T(8,128)}, f32[4,128,1]{1,2,0:T(1,128)}, s32[128]{0:T(128)S(1)}, /*ind...) while((s32[]{:T(128)}, bf16[4,1536,64]{2,1,0:T(8,128)(2,1)}, ...), condition=%wide.region_7.8_spmd, body=%wide.region_2.7_spmd.sunk | while | flops 243564560 | bytes 28432796 | solution.py:238
  223.3 8.9 all-gather.2
  232.2 10.0 all-gather.3
  242.2 14.4 %all-gather.4 = bf16[8,1,512]{2,1,0:T(2,128)(2,1)S(1)} all-gather(bf16[1,1,512]{2,1,0:T(2,128)(2,1)S(1)} %reshape.569), channel_id=1, replica_groups=mesh['seq'=4,'fsdp'=8] {'fsdp'}, dimensions={0}, use_global_device_ids=true | all-gather | bytes 9216 | tf_op jit(solution)/shard_map/all_gather | solution.py:208
  259.8 9.3 convolution_add_fusion
  272.1 11.9 convert_reduce_fusion
  309.5 333.8 %while.27 = (s32[]{:T(128)}, bf16[4,3,1536,64]{2,3,0,1:T(8,128)(2,1)}, s32[128]{0:T(128)S(1)}, s32[1536]{0:T(1024)S(1)}, bf16[4,1536,64]{2,1,0:T(8,128)(2,1)}, /...) while((s32[]{:T(128)}, ...), condition=%wide.region_17.18_spmd, body=%wide.region_12.17_spmd.sunk | while | flops 603952256 | bytes 75161568 | solution.py:305
  340.7 8.2 fusion.199
  349.0 18.4 %scatter_fusion.1 = f32[24,64,64]{2,1,0:T(8,128)S(1)} fusion(f32[24,64,64]{2,1,0:T(8,128)S(1)} %bitcast.293, s32[176]{0:T(256)S(1)} %reshape.624, f32[176,64,64]{2,1,0:T(8,128)} %bitcast.299), kind=kCustom, calls=%fused_computation.6.clone.1 | custom fusion | flops 720896 | bytes 8651456 | tf_op jit(solution)/shard_map/while/body/eval_jaxpr/scatter-add | solution.py:169
  372.7 18.4 %scatter_fusion = f32[24,64,64]{2,1,0:T(8,128)S(1)} fusion(f32[24,64,64]{2,1,0:T(8,128)S(1)} %bitcast.292, s32[176]{0:T(256)S(1)} %reshape.624, f32[176,64,64]{2,1,0:T(8,128)} %bitcast.298), kind=kCustom, calls=%fused_computation.7.clone.1 | custom fusion | flops 720896 | bytes 8651456 | tf_op jit(solution)/shard_map/while/body/eval_jaxpr/scatter-add | solution.py:172
  424.2 8.2 fusion.199
  432.4 18.4 %scatter_fusion.1 = f32[24,64,64]{2,1,0:T(8,128)S(1)} fusion(f32[24,64,64]{2,1,0:T(8,128)S(1)} %bitcast.293, s32[176]{0:T(256)S(1)} %reshape.624, f32[176,64,64]{2,1,0:T(8,128)} %bitcast.299), kind=kCustom, calls=%fused_computation.6.clone.1 | custom fusion | flops 720896 | bytes 8651456 | tf_op jit(solution)/shard_map/while/body/eval_jaxpr/scatter-add | solution.py:169
  456.2 18.4 %scatter_fusion = f32[24,64,64]{2,1,0:T(8,128)S(1)} fusion(f32[24,64,64]{2,1,0:T(8,128)S(1)} %bitcast.292, s32[176]{0:T(256)S(1)} %reshape.624, f32[176,64,64]{2,1,0:T(8,128)} %bitcast.298), kind=kCustom, calls=%fused_computation.7.clone.1 | custom fusion | flops 720896 | bytes 8651456 | tf_op jit(solution)/shard_map/while/body/eval_jaxpr/scatter-add | solution.py:172
  515.8 18.4 %scatter_fusion.1 = f32[24,64,64]{2,1,0:T(8,128)S(1)} fusion(f32[24,64,64]{2,1,0:T(8,128)S(1)} %bitcast.293, s32[176]{0:T(256)S(1)} %reshape.624, f32[176,64,64]{2,1,0:T(8,128)} %bitcast.299), kind=kCustom, calls=%fused_computation.6.clone.1 | custom fusion | flops 720896 | bytes 8651456 | tf_op jit(solution)/shard_map/while/body/eval_jaxpr/scatter-add | solution.py:169
  539.6 18.4 %scatter_fusion = f32[24,64,64]{2,1,0:T(8,128)S(1)} fusion(f32[24,64,64]{2,1,0:T(8,128)S(1)} %bitcast.292, s32[176]{0:T(256)S(1)} %reshape.624, f32[176,64,64]{2,1,0:T(8,128)} %bitcast.298), kind=kCustom, calls=%fused_computation.7.clone.1 | custom fusion | flops 720896 | bytes 8651456 | tf_op jit(solution)/shard_map/while/body/eval_jaxpr/scatter-add | solution.py:172
  599.2 18.4 %scatter_fusion.1 = f32[24,64,64]{2,1,0:T(8,128)S(1)} fusion(f32[24,64,64]{2,1,0:T(8,128)S(1)} %bitcast.293, s32[176]{0:T(256)S(1)} %reshape.624, f32[176,64,64]{2,1,0:T(8,128)} %bitcast.299), kind=kCustom, calls=%fused_computation.6.clone.1 | custom fusion | flops 720896 | bytes 8651456 | tf_op jit(solution)/shard_map/while/body/eval_jaxpr/scatter-add | solution.py:169
  623.0 18.4 %scatter_fusion = f32[24,64,64]{2,1,0:T(8,128)S(1)} fusion(f32[24,64,64]{2,1,0:T(8,128)S(1)} %bitcast.292, s32[176]{0:T(256)S(1)} %reshape.624, f32[176,64,64]{2,1,0:T(8,128)} %bitcast.298), kind=kCustom, calls=%fused_computation.7.clone.1 | custom fusion | flops 720896 | bytes 8651456 | tf_op jit(solution)/shard_map/while/body/eval_jaxpr/scatter-add | solution.py:172
  647.5 38.9 %all_to_all.62 = bf16[1536,3,256]{2,1,0:T(4,128)(2,1)S(1)} all-to-all(bf16[1536,3,256]{2,1,0:T(4,128)(2,1)S(1)} %copy.189), channel_id=1, replica_groups=mesh['seq'=4,'fsdp'=8] {'seq'}, dimensions={0} | all-to-all | bytes 4718592 | tf_op jit(solution)/shard_map/all_to_all | solution.py:310
  699.3 12.4 fusion.78
  713.1 10.2 fusion.95
  723.3 101.3 %reduce-scatter.5.cloned.1.call-done = f32[128,3072]{1,0:T(8,128)} async-done(((f32[1024,3072]{1,0:T(8,128)}), f32[128,3072]{1,0:T(8,128)}) %reduce-scatter.5.cloned.1.call-update) | async-done | bytes 1572880 | tf_op jit(solution)/shard_map/reduce_scatter | solution.py:320
  824.7 169.0 %reduce-scatter.11.cloned.1.call-done = f32[512,1024]{1,0:T(8,128)} async-done(((f32[4096,1024]{1,0:T(8,128)}), f32[512,1024]{1,0:T(8,128)}) %reduce-scatter.11.cloned.1.call-update) | async-done | bytes 2097168 | tf_op jit(solution)/shard_map/reduce_scatter | solution.py:279
  993.6 169.0 %reduce-scatter.9.cloned.1.call-done = f32[128,4096]{1,0:T(8,128)} async-done(((f32[1024,4096]{1,0:T(8,128)}), f32[128,4096]{1,0:T(8,128)}) %reduce-scatter.9.cloned.1.call-update) | async-done | bytes 2097168 | tf_op jit(solution)/shard_map/reduce_scatter | solution.py:277
  1165.2 9.3 all-gather.5
  1174.5 10.5 fusion.71
  1193.4 26.7 %all-reduce.6 = (f32[1024]{0:T(1024)S(1)}, f32[1024]{0:T(1024)S(1)}, f32[1024]{0:T(1024)S(1)}, f32[1024]{0:T(1024)S(1)}, f32[4096]{0:T(1024)S(1)}, /*index=5*/f32[1024]{0:T(1024)S(1)}) all-reduce(f32[1024]{0:T(1024)S(1)} %get-tuple-element.315, f32[1024]{0:T(1024)S(1)} %get-tuple-element.318, ...), channel_id=2, replica_groups=mesh['seq'=4,'fsdp'=8] {'fsdp'}, use_global_device_ids=true, to_apply=%region_21.22.clone | all-reduce | flops 9216 | bytes 73728
  1220.6 11.4 all-reduce.7
  1232.0 72.6 %all-reduce.11.cloned.1.call-done = (f32[128,3072]{1,0:T(8,128)}, f32[128,1024]{1,0:T(8,128)}, f32[128,4096]{1,0:T(8,128)}, f32[512,1024]{1,0:T(8,128)}) async-done(((f32[128,3072]{1,0:T(8,128)}, f32[128,1024]{1,0:T(8,128)}, f32[128,4096]{1,0:T(8,128)}, f32[512,1024]{1,0:T(8,128)}), (f32[128,3072]{1,0:T(8,128)}, f32[128,1024]{1,0:T(8,128)}, f32[128,4096]{1,0:T(8,128)}, ...) | async-done | bytes 6291472 | tf_op jit(solution)/shard_map/psum | solution.py:324
  (591 shorter events, 352.4 us)
Async XLA Ops:
  7.2 19.2 %copy-start.56 = (bf16[128]{0:T(256)(128)(2,1)S(1)}, bf16[128]{0:T(256)(128)(2,1)}, u32[]{:S(2)}) copy-start(bf16[128]{0:T(256)(128)(2,1)} %param.22) | copy-start | bytes 772
  7.2 70.0 %all-gather.11.cloned.1.call-start = ((), (), s32[]{:S(2)}) async-start(), calls=%async_computation.8 | async-start | bytes 7077888 | tf_op jit(solution)/shard_map/all_gather | solution.py:201
  7.9 248.8 %all-gather.13.cloned.1.call-start = ((), (), s32[]{:S(2)}) async-start(), calls=%async_computation.9 | async-start | bytes 2359296 | tf_op jit(solution)/shard_map/all_gather | solution.py:202
  8.7 251.1 %all-gather.15.cloned.1.call-start = ((), (), s32[]{:S(2)}) async-start(), calls=%async_computation.10 | async-start | bytes 9437184 | tf_op jit(solution)/shard_map/all_gather | solution.py:207
  9.4 262.7 %all-gather.17.cloned.1.call-start = ((), (), s32[]{:S(2)}) async-start(), calls=%async_computation.11 | async-start | bytes 9437184 | tf_op jit(solution)/shard_map/all_gather | solution.py:209
  10.2 84.6 %collective-permute-start = (s32[384]{0:T(512)S(1)}, s32[384]{0:T(512)S(1)}, u32[]{:S(2)}, u32[]{:S(2)}) collective-permute-start(s32[384]{0:T(512)S(1)} %reduce.1), channel_id=1, source_target_pairs={{0,8},{8,16},{16,24},{24,0},{1,9},{9,17},{17,25},{25,1},{2,10},{10... | collective-permute-start | bytes 4616 | tf_op jit(solution)/shard_map/ppermute | solution.py:226
  13.4 63.8 %copy-start.37 = (f32[384]{0:T(512)}, f32[384]{0:T(512)S(1)}, u32[]{:S(2)}) copy-start(f32[384]{0:T(512)S(1)} %broadcast_multiply_fusion.1) | copy-start | bytes 4612
  13.8 63.5 %copy-start.41 = (f32[384]{0:T(512)}, f32[384]{0:T(512)S(1)}, u32[]{:S(2)}) copy-start(f32[384]{0:T(512)S(1)} %fusion.92) | copy-start | bytes 4612
  26.3 50.9 %copy-start.31 = (f32[8,1,128]{2,1,0:T(1,128)}, f32[8,1,128]{2,1,0:T(1,128)S(1)}, u32[]{:S(2)}) copy-start(f32[8,1,128]{2,1,0:T(1,128)S(1)} %convert_element_type.130) | copy-start | bytes 12292
  35.2 42.1 %copy-start.33 = (f32[8,1,128]{2,1,0:T(1,128)}, f32[8,1,128]{2,1,0:T(1,128)S(1)}, u32[]{:S(2)}) copy-start(f32[8,1,128]{2,1,0:T(1,128)S(1)} %convert_element_type.131) | copy-start | bytes 12292
  90.8 41.7 %copy-start.54 = (s32[22,2]{0,1:T(2,128)S(1)}, s32[22,2]{0,1:T(2,128)}, u32[]{:S(2)}) copy-start(s32[22,2]{0,1:T(2,128)} %constant.128.clone.1) | copy-start | bytes 532
  90.8 46.5 %all-to-all-start = ((bf16[384,3,1024]{0,1,2:T(4,128)(2,1)}), bf16[384,3,1024]{0,1,2:T(4,128)(2,1)S(1)}, u32[]{:S(2)}, u32[]{:S(2)}) async-start(bf16[384,3,1024]{0,1,2:T(4,128)(2,1)} %copy.169), calls=%async_computation | async-start | bytes 6291456 | tf_op jit(solution)/shard_map/all_to_all | solution.py:223
  94.7 37.6 %collective-permute-start.1 = (s32[384]{0:T(512)S(1)}, s32[384]{0:T(512)S(1)}, u32[]{:S(2)}, u32[]{:S(2)}) collective-permute-start(s32[384]{0:T(512)S(1)} %collective-permute-done), channel_id=1, source_target_pairs={{0,8},{8,16},{16,24},{24,0},{1,9},{9,17},{17,25},{25,1},{2,10},{10... | collective-permute-start | bytes 4616 | tf_op jit(solution)/shard_map/ppermute | solution.py:226
  132.4 4.6 collective-permute-start.2
  218.5 13.7 %copy-start.58 = (bf16[128]{0:T(256)(128)(2,1)S(1)}, bf16[128]{0:T(256)(128)(2,1)}, u32[]{:S(2)}) copy-start(bf16[128]{0:T(256)(128)(2,1)} %param.26) | copy-start | bytes 772
  218.6 38.2 %copy-start.3 = (bf16[1,384,1024]{2,1,0:T(8,128)(2,1)S(1)}, bf16[1,384,1024]{2,1,0:T(8,128)(2,1)}, u32[]{:S(2)}) copy-start(bf16[1,384,1024]{2,1,0:T(8,128)(2,1)} %param.18) | copy-start | bytes 2359300
  219.7 37.0 %all-to-all-start.1 = ((bf16[4,384,256]{1,2,0:T(8,128)(2,1)}), bf16[4,384,256]{1,2,0:T(8,128)(2,1)S(1)}, u32[]{:S(2)}, u32[]{:S(2)}) async-start(bf16[4,384,256]{1,2,0:T(8,128)(2,1)} %copy.179), calls=%async_computation.1 | async-start | bytes 1572864 | tf_op jit(solution)/shard_map/all_to_all | solution.py:242
  232.2 56.1 %copy-start.22 = (f32[8,1,128]{2,1,0:T(1,128)}, f32[8,1,128]{2,1,0:T(1,128)S(1)}, u32[]{:S(2)}) copy-start(f32[8,1,128]{2,1,0:T(1,128)S(1)} %convert_element_type.132) | copy-start | bytes 12292
  242.2 17.6 %copy-start.26 = (f32[8,1,128]{2,1,0:T(1,128)}, f32[8,1,128]{2,1,0:T(1,128)S(1)}, u32[]{:S(2)}) copy-start(f32[8,1,128]{2,1,0:T(1,128)S(1)} %convert_element_type.133) | copy-start | bytes 12292
  259.4 29.0 %copy-start.5 = (f32[384,1024]{1,0:T(8,128)}, f32[384,1024]{1,0:T(8,128)S(1)}, u32[]{:S(2)}) copy-start(f32[384,1024]{1,0:T(8,128)S(1)} %get-tuple-element.416) | copy-start | bytes 4718596
  259.4 28.9 %copy-start.35 = (f32[384]{0:T(512)}, f32[384]{0:T(512)S(1)}, u32[]{:S(2)}) copy-start(f32[384]{0:T(512)S(1)} %broadcast_multiply_fusion) | copy-start | bytes 4612
  259.7 28.6 %copy-start.39 = (f32[384]{0:T(512)}, f32[384]{0:T(512)S(1)}, u32[]{:S(2)}) copy-start(f32[384]{0:T(512)S(1)} %fusion.93) | copy-start | bytes 4612
  259.8 12.3 copy-start.12
  272.1 11.9 copy-start.60
  292.7 15.0 %all-to-all-start.2 = ((bf16[384,4,256]{0,2,1:T(8,128)(2,1)}), bf16[384,4,256]{0,2,1:T(8,128)(2,1)S(1)}, u32[]{:S(2)}, u32[]{:S(2)}) async-start(bf16[384,4,256]{0,2,1:T(8,128)(2,1)} %bitcast.61), calls=%async_computation.2 | async-start | bytes 1572864 | tf_op jit(solution)/shard_map/all_to_all | solution.py:289
  296.4 427.0 %reduce-scatter.7.cloned.1.call-start = ((), (), s32[]{:S(2)}) async-start(), calls=%async_computation.13 | async-start | bytes 4718592 | tf_op jit(solution)/shard_map/reduce_scatter | solution.py:321
  299.6 525.0 %reduce-scatter.5.cloned.1.call-start = ((), (), s32[]{:S(2)}) async-start(), calls=%async_computation.12 | async-start | bytes 14155776 | tf_op jit(solution)/shard_map/reduce_scatter | solution.py:320
  309.5 10.7 copy-start.48
  393.0 10.7 copy-start.48
  698.1 295.5 %reduce-scatter.11.cloned.1.call-start = ((), (), s32[]{:S(2)}) async-start(), calls=%async_computation.15 | async-start | bytes 18874368 | tf_op jit(solution)/shard_map/reduce_scatter | solution.py:279
  711.7 450.9 %reduce-scatter.9.cloned.1.call-start = ((), (), s32[]{:S(2)}) async-start(), calls=%async_computation.14 | async-start | bytes 18874368 | tf_op jit(solution)/shard_map/reduce_scatter | solution.py:277
  723.3 581.4 %all-reduce.11.cloned.1.call-start = ((), (), s32[]{:S(2)}) async-start(), calls=%async_computation.16 | async-start | bytes 12582912 | tf_op jit(solution)/shard_map/psum | solution.py:324
  (81 other events, 325.5 us)
Sparse Core Ops, SparseCore 0:
  9.7 67.4 all-gather.10
  78.8 27.6 all-gather.12
  108.2 81.6 all-gather.14
  191.3 80.7 all-gather.16
  299.8 49.0 reduce-scatter.6
  698.3 126.3 reduce-scatter.4
  827.0 166.5 reduce-scatter.10
  996.0 166.5 reduce-scatter.8
  1166.4 138.2 all-reduce.10
